TPU v7x, 512 devices: a whole 4x4x16 slice. The times are simulated.
512 devices in a mesh: batch: 32 (over z, core), row: 4 (over y), col: 4 (over x).
Axes of the slice: x: 4, y: 4, z: 16, core: 2. Of those that a mesh axis runs over, the one named last changes fastest.
Arguments:
- image_tokens: bfloat16 [128, 256, 3072], P('batch', ('row', 'col')), may hold values from -36 to 36
- text_tokens: bfloat16 [128, 128, 3072], P('batch', ('row', 'col')), may hold values from -36 to 36
- modulation: float32 [128, 7, 3072], P('batch'), may hold values from -3.5 to 3.5
- qkv_weight: bfloat16 [3072, 12, 384], P('col', 'row'), may hold values from -0.109375 to 0.109375
- kv_weight: bfloat16 [3072, 12, 256], P('col', 'row'), may hold values from -0.109375 to 0.109375
- norm_gains: float32 [3, 128], replicated, may hold values from 1 to 2.2
- out_weight: bfloat16 [12, 128, 3072], P('row', None, 'col'), may hold values from -0.15625 to 0.15625
- final_weight: bfloat16 [3072, 64], replicated, may hold values from -0.109375 to 0.109375
- text_lengths: int32 [128], P('batch'), may hold values from 1 to 128, as said below
- partner: int32 [128], P('batch'), may hold values from 0 to 127, as said below
- guidance: float32 [128], P('batch'), may hold values from 1.5 to 4.5
- step_size: float32 [128], P('batch'), may hold values from -0.3 to -0.05
- latent: float32 [128, 256, 64], P('batch', ('row', 'col')), may hold values from -6 to 6
Outputs:
- next_latent: float32 [128, 256, 64], P('batch', ('row', 'col'))
Inputs may be any that keep to these rules, and one draw needn't show every extreme that they name: `text_lengths`: some sequence has all 128 text tokens live. partner[partner[s]] = s and partner[s] != s for every sequence s.
All inputs are finite; a program needn't handle non-finite values.
Results may differ from a plain program's by a relative error of at most 0.007.
Values may be sent and summed in bfloat16 or wider, within the bound.
No kernel may reach another device: no remote copies, remote signals or barrier semaphores. Data moves between devices by JAX's collectives and lax.ppermute only.
A program may use at most 64 MiB of HBM per device.

v0:
```python
import math
import jax
import jax.numpy as jnp
from jax import lax
from jax.sharding import PartitionSpec as P

epsilon = 1e-06


def layer_norm(values):
    center = jnp.mean(values, axis=-1, keepdims=True)
    spread = jnp.mean((values - center) * (values - center), axis=-1, keepdims=True)
    return (values - center) * lax.rsqrt(spread + epsilon)


def modulate(values, shift, scale):
    return layer_norm(values) * (1.0 + scale[:, None, :]) + shift[:, None, :]


def head_norm(values, gain):
    return values * lax.rsqrt(jnp.mean(values * values, axis=-1, keepdims=True) + epsilon) * gain


def attend(queries, all_keys, all_values, live, head_size):
    scores = jnp.einsum(
        "sqhe,skhe->shqk", queries, all_keys, preferred_element_type=jnp.float32
    ) / math.sqrt(head_size)
    expo = jnp.exp(scores) * live[:, None, None, :]
    totals = jnp.sum(expo, axis=-1)
    mixed = jnp.einsum(
        "shqk,skhe->sqhe", expo.astype(jnp.bfloat16), all_values, preferred_element_type=jnp.float32
    )
    return (mixed / jnp.transpose(totals, (0, 2, 1))[..., None]).astype(jnp.bfloat16)


def per_device(
    image_tokens,
    text_tokens,
    modulation,
    qkv_weight,
    kv_weight,
    norm_gains,
    out_weight,
    final_weight,
    text_lengths,
    partner,
    guidance,
    step_size,
    latent,
):
    count = image_tokens.shape[0]
    head_size = norm_gains.shape[1]
    block_width = qkv_weight.shape[0]
    image_mod = modulate(
        image_tokens.astype(jnp.float32), modulation[:, 0], modulation[:, 1]
    ).astype(jnp.bfloat16)
    text_mod = modulate(text_tokens.astype(jnp.float32), modulation[:, 3], modulation[:, 4]).astype(
        jnp.bfloat16
    )
    image_whole, text_whole = (
        lax.all_gather(image_mod, ("row", "col"), axis=1, tiled=True),
        lax.all_gather(text_mod, ("row", "col"), axis=1, tiled=True),
    )
    offset = lax.axis_index("col") * block_width
    image_all = lax.dynamic_slice_in_dim(image_whole, offset, block_width, 2)
    text_all = lax.dynamic_slice_in_dim(text_whole, offset, block_width, 2)
    qkv_term = jnp.einsum(
        "std,dhe->sthe", image_all, qkv_weight, preferred_element_type=jnp.float32
    )
    kv_term = jnp.einsum("std,dhe->sthe", text_all, kv_weight, preferred_element_type=jnp.float32)
    qkv_sum, kv_sum = (
        lax.psum(qkv_term.astype(jnp.bfloat16), "col").astype(jnp.float32),
        lax.psum(kv_term.astype(jnp.bfloat16), "col").astype(jnp.float32),
    )
    queries = head_norm(qkv_sum[..., :head_size], norm_gains[0]).astype(jnp.bfloat16)
    image_keys = head_norm(qkv_sum[..., head_size : 2 * head_size], norm_gains[1]).astype(
        jnp.bfloat16
    )
    image_values = qkv_sum[..., 2 * head_size :].astype(jnp.bfloat16)
    text_keys = head_norm(kv_sum[..., :head_size], norm_gains[2]).astype(jnp.bfloat16)
    text_values = kv_sum[..., head_size:].astype(jnp.bfloat16)
    text_count = text_keys.shape[1]
    image_count = image_keys.shape[1]
    all_keys = jnp.concatenate([text_keys, image_keys], axis=1)
    all_values = jnp.concatenate([text_values, image_values], axis=1)
    text_live = (jnp.arange(text_count, dtype=jnp.int32)[None, :] < text_lengths[:, None]).astype(
        jnp.float32
    )
    live = jnp.concatenate([text_live, jnp.ones((count, image_count), jnp.float32)], axis=1)
    heads = attend(queries, all_keys, all_values, live, head_size)
    out_term = jnp.einsum("sqhe,hed->sqd", heads, out_weight, preferred_element_type=jnp.float32)
    attn_rows = lax.psum_scatter(
        out_term.astype(jnp.bfloat16), "row", scatter_dimension=1, tiled=True
    )
    attn_tokens = lax.all_to_all(attn_rows, "col", split_axis=1, concat_axis=2, tiled=True)
    residual = image_tokens.astype(jnp.float32) + modulation[:, 2][:, None, :] * attn_tokens.astype(
        jnp.float32
    )
    final_in = modulate(residual, modulation[:, 5], modulation[:, 6]).astype(jnp.bfloat16)
    velocity = jnp.einsum("std,dc->stc", final_in, final_weight, preferred_element_type=jnp.float32)
    token_rows = velocity.shape[1]
    channels = velocity.shape[2]
    flat_velocity = velocity.reshape(count, token_rows * channels)
    every_velocity, every_guidance = (
        lax.all_gather(flat_velocity, "batch", axis=0, tiled=True),
        lax.all_gather(guidance, "batch", axis=0, tiled=True),
    )
    mate = jnp.take(every_velocity, partner, axis=0).reshape(velocity.shape)
    own_index = lax.axis_index("batch") * count + jnp.arange(count, dtype=jnp.int32)
    is_cond = own_index < partner
    cond_vel = jnp.where(is_cond[:, None, None], velocity, mate)
    uncond_vel = jnp.where(is_cond[:, None, None], mate, velocity)
    scale_guide = jnp.where(is_cond, guidance, jnp.take(every_guidance, partner))
    guided = uncond_vel + scale_guide[:, None, None] * (cond_vel - uncond_vel)
    ratio = jnp.sqrt(
        (jnp.mean(cond_vel * cond_vel, axis=-1, keepdims=True) + epsilon)
        / (jnp.mean(guided * guided, axis=-1, keepdims=True) + epsilon)
    )
    return latent + step_size[:, None, None] * guided * (0.7 * ratio + 0.3)


def solution(mesh):
    return jax.shard_map(
        per_device,
        mesh=mesh,
        in_specs=(
            P("batch", ("row", "col"), None),
            P("batch", ("row", "col"), None),
            P("batch", None, None),
            P("col", "row", None),
            P("col", "row", None),
            P(),
            P("row", None, "col"),
            P(),
            P("batch"),
            P("batch"),
            P("batch"),
            P("batch"),
            P("batch", ("row", "col"), None),
        ),
        out_specs=P("batch", ("row", "col"), None),
        check_vma=False,
    )
```

profile of v0, /device:TPU:1, one launch (start us, length us, event | category | flops | bytes accessed | tf_op | source)
XLA Modules:
  0.0 376.6 jit_solution(10970847019949007939)
XLA Ops:
  6.5 1.2 convert_reduce_fusion.1
  7.7 1.1 fusion.42
  8.9 1.0 slice_bitcast_fusion.3
  9.9 1.8 fusion.45
  11.7 1.1 convert_reduce_fusion
  13.1 1.0 fusion.30
  14.2 65.4 %all-gather.4.cloned.1.call-done = bf16[4,128,3072]{2,1,0:T(8,128)(2,1)} async-done(((bf16[4,8,3072]{2,1,0:T(8,128)(2,1)}), bf16[4,128,3072]{2,1,0:T(8,128)(2,1)}) %all-gather.4.cloned.1.call-update) | async-done | bytes 3145744 | tf_op jit(solution)/shard_map/all_gather | solution.py:62
  79.6 3.2 convolution_convert_fusion.1
  82.7 75.8 %all-gather.6.cloned.1.call-done = bf16[4,256,3072]{2,1,0:T(8,128)(2,1)} async-done(((bf16[4,16,3072]{2,1,0:T(8,128)(2,1)}), bf16[4,256,3072]{2,1,0:T(8,128)(2,1)}) %all-gather.6.cloned.1.call-update) | async-done | bytes 6291472 | tf_op jit(solution)/shard_map/all_gather | solution.py:61
  158.5 5.0 %convolution_convert_fusion = bf16[4,256,3,384]{3,1,2,0:T(8,128)(2,1)} fusion(bf16[768,3,384]{2,0,1:T(8,128)(2,1)S(1)} %copy-done, bf16[4,256,3072]{2,1,0:T(8,128)(2,1)} %all-gather.6.cloned.1.call-done, s32[]{:T(128)S(6)} %select_n.32), kind=kOutput, calls=%fused_computation.9 | convolution fusion | flops 1813118976 | bytes 5701636 | tf_op jit(solution)/shard_map/std,dhe->sthe/dot_general | solution.py:67
  163.6 0.6 copy-done.9
  164.3 90.3 %all-reduce.5.cloned.1.call-done = (bf16[4,256,3,384]{3,1,2,0:T(8,128)(2,1)}, bf16[4,128,3,256]{3,1,2,0:T(8,128)(2,1)}) async-done(((bf16[4,256,3,384]{3,1,2,0:T(8,128)(2,1)}, bf16[4,128,3,256]{3,1,2,0:T(8,128)(2,1)}), (bf16[4,256,3,384]{3,1,2,0:T(8,128)(2,1)}, bf16[4,128,3,256]{3,1,2,0:T(8,128)(2,1)})) %all-reduce.5.cloned.1.call-update) | async-done | bytes 3145744 | tf_op jit(solution)/shard_map/psum | solution.py:72
  254.6 1.4 fusion.31
  256.0 1.0 slice.70
  257.1 1.2 slice.71
  258.3 0.4 convert_element_type.65
  258.7 0.9 multiply_reduce_fusion.1
  260.2 0.5 multiply_convert_fusion
  260.6 2.8 fusion
  263.4 5.8 %bitcast_convert_fusion = bf16[4,256,768]{2,1,0:T(8,128)(2,1)} fusion(f32[4,3,256,384]{3,2,1,0:T(8,128)} %get-tuple-element.25, f32[4,384]{1,0:T(4,128)S(1)} %pad_convert_fusion, bf16[4,256,3,128]{3,1,2,0:T(8,128)(2,1)S(1)} %slice.71, bf16[4,128,3,128]{3,1,2,0:T(8,128)(2,1)S(1)} %slice.70, f32[4,256,3]{1,2,0:T(4,128)S(1)} %bitcast.60, ...), kind=kOutput, calls=%fused_computation.5 | convolution fusion | flops 913440768 | bytes 8079360 | tf_op jit(solution)/shard_map/sqhe,hed->sqd/dot_general | solution.py:91
  269.2 1.3 dynamic-slice
  271.4 48.1 %all-reduce.1 = f32[128]{0:T(128)S(1)} all-reduce(f32[128]{0:T(128)S(1)} %dynamic-update-slice), channel_id=1, replica_groups=mesh['batch'=32,'row'=4,'col'=4] {'batch'}, use_global_device_ids=true, to_apply=%add.1 | all-reduce | flops 128 | bytes 1024
  319.6 2.0 copy.18
  321.6 3.5 all-to-all-start
  325.1 0.6 gather_fusion.1
  325.8 5.5 %all-to-all-done = bf16[4,64,768]{2,0,1:T(4,128)(2,1)S(1)} async-done(((bf16[4,64,768]{2,0,1:T(4,128)(2,1)}), bf16[4,64,768]{2,0,1:T(4,128)(2,1)S(1)}, u32[]{:S(2)}, u32[]{:S(2)}) %all-to-all-start) | async-done | bytes 393248 | tf_op jit(solution)/shard_map/all_to_all | solution.py:95
  331.3 1.2 copy.26
  332.5 1.5 reshape.109
  334.5 1.4 fusion.46
  336.0 32.3 %all-gather = f32[32,4,1024]{2,1,0:T(4,128)S(1)} all-gather(f32[1,4,1024]{2,1,0:T(4,128)S(1)} %reshape.132), channel_id=1, replica_groups=mesh['batch'=32,'row'=4,'col'=4] {'batch'}, dimensions={0}, use_global_device_ids=true | all-gather | bytes 540672 | tf_op jit(solution)/shard_map/all_gather | solution.py:105
  368.5 0.6 gather_fusion
  369.4 0.7 multiply_add_fusion
  (54 shorter events, 2.4 us)
Async XLA Ops:
  6.5 152.0 %copy-start = (bf16[768,3,384]{2,0,1:T(8,128)(2,1)S(1)}, bf16[768,3,384]{2,0,1:T(8,128)(2,1)}, u32[]{:S(2)}) copy-start(bf16[768,3,384]{2,0,1:T(8,128)(2,1)} %param.16) | copy-start | bytes 5308420
  6.5 6.3 %copy-start.1 = (bf16[4,16,3072]{2,1,0:T(8,128)(2,1)S(1)}, bf16[4,16,3072]{2,1,0:T(8,128)(2,1)}, u32[]{:S(2)}) copy-start(bf16[4,16,3072]{2,1,0:T(8,128)(2,1)} %param.13) | copy-start | bytes 1179652
  6.5 73.0 %all-gather.4.cloned.1.call-start = ((), (), s32[]{:S(2)}) async-start(), calls=%async_computation.2 | async-start | bytes 3342336 | tf_op jit(solution)/shard_map/all_gather | solution.py:62
  11.7 146.9 %all-gather.6.cloned.1.call-start = ((), (), s32[]{:S(2)}) async-start(), calls=%async_computation.3 | async-start | bytes 6684672 | tf_op jit(solution)/shard_map/all_gather | solution.py:61
  14.1 240.5 %all-reduce.5.cloned.1.call-start = ((), (), s32[]{:S(2)}) async-start(), calls=%async_computation.5 | async-start | bytes 6291456 | tf_op jit(solution)/shard_map/psum | solution.py:72
  163.5 0.7 copy-start.9
  163.5 0.7 copy-start.5
  163.6 156.0 %reduce-scatter.2.cloned.1.call-start = ((), (), s32[]{:S(2)}) async-start(), calls=%async_computation.4 | async-start | bytes 1966080 | tf_op jit(solution)/shard_map/reduce_scatter | solution.py:92
  254.6 3.7 copy-start.2
  258.7 1.1 copy-start.3
  263.4 7.7 %copy-start.7 = (f32[4]{0:T(128)S(1)}, f32[4]{0:T(128)}, u32[]{:S(2)}) copy-start(f32[4]{0:T(128)} %param.23) | copy-start | bytes 52
  263.4 56.1 %copy-start.8 = (s32[4]{0:T(128)S(1)}, s32[4]{0:T(128)}, u32[]{:S(2)}) copy-start(s32[4]{0:T(128)} %param.22) | copy-start | bytes 52
  321.6 9.7 %all-to-all-start = ((bf16[4,64,768]{2,0,1:T(4,128)(2,1)}), bf16[4,64,768]{2,0,1:T(4,128)(2,1)S(1)}, u32[]{:S(2)}, u32[]{:S(2)}) async-start(bf16[4,64,768]{2,0,1:T(4,128)(2,1)} %copy.18), calls=%async_computation.1 | async-start | bytes 786432 | tf_op jit(solution)/shard_map/all_to_all | solution.py:95
  334.2 35.1 %copy-start.4 = (f32[4,16,64]{2,1,0:T(8,128)S(1)}, f32[4,16,64]{2,1,0:T(8,128)}, u32[]{:S(2)}) copy-start(f32[4,16,64]{2,1,0:T(8,128)} %param.25) | copy-start | bytes 49156
  334.2 35.1 %copy-start.6 = (f32[4]{0:T(128)S(1)}, f32[4]{0:T(128)}, u32[]{:S(2)}) copy-start(f32[4]{0:T(128)} %param.24) | copy-start | bytes 52
Sparse Core Ops, SparseCore 0:
  11.8 67.7 all-gather.3
  82.6 75.8 all-gather.5
  163.7 90.8 all-reduce.4
  269.3 32.5 reduce-scatter.1
where the time goes:
time: 377 us
  waiting for transfers between devices  237 us (63%)
  blocking collectives  80.4 us (21%)
  matrix products  18.2 us (5%)
  between operations  14 us (4%)
  other arithmetic  12.5 us (3%)
  local copies, waits for them, and re-layouts  10.9 us (3%)
    psum x1, waiting for transfers between devices, per_device(): lax.psum(qkv_term.astype(jnp.bfloat16), 'col').astype(jnp.float32)  90.3 us
    all_gather x1, waiting for transfers between devices, per_device(): lax.all_gather(image_mod, ('row', 'col'), axis=1, tiled=True)  75.8 us
    all_gather x1, waiting for transfers between devices, per_device(): lax.all_gather(text_mod, ('row', 'col'), axis=1, tiled=True)  65.4 us
    unnamed x1, blocking collectives  48.1 us
    all_gather x1, blocking collectives, per_device(): lax.all_gather(flat_velocity, 'batch', axis=0, tiled=True)  32.3 us
  transfers between devices with their start and end apart: 5, of which 4 were waited for; matrix products, arithmetic and copies ran while one was open for 2% of the time, Pallas kernels for 0%

commit v1 on v0

--- a/solution.py
+++ b/solution.py
@@ -102,7 +102,10 @@
     channels = velocity.shape[2]
     flat_velocity = velocity.reshape(count, token_rows * channels)
     every_velocity, every_guidance = (
-        lax.all_gather(flat_velocity, "batch", axis=0, tiled=True),
+        jnp.concatenate(
+            lax.all_to_all(jnp.stack([flat_velocity] * lax.axis_size("batch")), "batch", 0, 0),
+            axis=0,
+        ),
         lax.all_gather(guidance, "batch", axis=0, tiled=True),
     )
     mate = jnp.take(every_velocity, partner, axis=0).reshape(velocity.shape)

time: 377 us -> 408 us (1.082)
  waiting for transfers between devices: 237 us -> 264 us
  starting transfers between devices: 3.59 us -> 15.5 us
  blocking collectives: 80.4 us -> 71.7 us
    reduce_scatter x1, waiting for transfers between devices: 0.02 us -> 32.7 us  [per_device(): lax.psum_scatter(out_term.astype(jnp.bfloat16), 'row', scatter_dimension=...]
    all_gather x1 -> x0, blocking collectives: 32.3 us -> none  [per_device(): lax.all_gather(flat_velocity, 'batch', axis=0, tiled=True)]
    unnamed x1, blocking collectives: 48.1 us -> 61.7 us
    all_to_all x1, starting transfers between devices: 3.46 us -> 15.3 us  [per_device(): lax.all_to_all(jnp.stack([flat_velocity] * lax.axis_size('batch')), 'batc...]
    all_to_all x0 -> x1, blocking collectives: none -> 10 us  [per_device(): lax.all_to_all(attn_rows, 'col', split_axis=1, concat_axis=2, tiled=True)]
    all_to_all x1, waiting for transfers between devices: 5.53 us -> 0.01 us  [per_device(): lax.all_to_all(jnp.stack([flat_velocity] * lax.axis_size('batch')), 'batc...]
where the time goes in v1:
time: 408 us; the launch traced here: 407 us
  waiting for transfers between devices  264 us (65%)
  blocking collectives  71.7 us (18%)
  matrix products  18.1 us (4%)
  starting transfers between devices  15.5 us (4%)
  between operations  14 us (3%)
  other arithmetic  12.4 us (3%)
  local copies, waits for them, and re-layouts  11 us (3%)
    psum x1, waiting for transfers between devices, per_device(): lax.psum(qkv_term.astype(jnp.bfloat16), 'col').astype(jnp.float32)  90.3 us
    all_gather x1, waiting for transfers between devices, per_device(): lax.all_gather(image_mod, ('row', 'col'), axis=1, tiled=True)  75.8 us
    all_gather x1, waiting for transfers between devices, per_device(): lax.all_gather(text_mod, ('row', 'col'), axis=1, tiled=True)  65.4 us
    unnamed x1, blocking collectives  61.7 us
    reduce_scatter x1, waiting for transfers between devices, per_device(): lax.psum_scatter(out_term.astype(jnp.bfloat16), 'row', scatter_dimension=...  32.7 us
    all_to_all x1, starting transfers between devices, per_device(): lax.all_to_all(jnp.stack([flat_velocity] * lax.axis_size('batch')), 'batc...  15.3 us
    all_to_all x1, blocking collectives, per_device(): lax.all_to_all(attn_rows, 'col', split_axis=1, concat_axis=2, tiled=True)  10 us
  transfers between devices with their start and end apart: 5, of which 4 were waited for; matrix products, arithmetic and copies ran while one was open for 2% of the time, Pallas kernels for 0%

profile of v1, /device:TPU:1, one launch (start us, length us, event | category | flops | bytes accessed | tf_op | source)
XLA Modules:
  0.0 407.1 jit_solution(13255461365807404248)
XLA Ops:
  6.5 1.2 convert_reduce_fusion.1
  7.7 1.1 fusion.42
  8.9 1.0 slice_bitcast_fusion.3
  9.9 1.8 fusion.45
  11.7 1.1 convert_reduce_fusion
  13.1 1.0 fusion.30
  14.2 65.4 %all-gather.3.cloned.1.call-done = bf16[4,128,3072]{2,1,0:T(8,128)(2,1)} async-done(((bf16[4,8,3072]{2,1,0:T(8,128)(2,1)}), bf16[4,128,3072]{2,1,0:T(8,128)(2,1)}) %all-gather.3.cloned.1.call-update) | async-done | bytes 3145744 | tf_op jit(solution)/shard_map/all_gather | solution.py:62
  79.6 3.2 convolution_convert_fusion.1
  82.7 75.8 %all-gather.5.cloned.1.call-done = bf16[4,256,3072]{2,1,0:T(8,128)(2,1)} async-done(((bf16[4,16,3072]{2,1,0:T(8,128)(2,1)}), bf16[4,256,3072]{2,1,0:T(8,128)(2,1)}) %all-gather.5.cloned.1.call-update) | async-done | bytes 6291472 | tf_op jit(solution)/shard_map/all_gather | solution.py:61
  158.5 5.0 %convolution_convert_fusion = bf16[4,256,3,384]{3,1,2,0:T(8,128)(2,1)} fusion(bf16[768,3,384]{2,0,1:T(8,128)(2,1)S(1)} %copy-done, bf16[4,256,3072]{2,1,0:T(8,128)(2,1)} %all-gather.5.cloned.1.call-done, s32[]{:T(128)S(6)} %select_n.32), kind=kOutput, calls=%fused_computation.9 | convolution fusion | flops 1813118976 | bytes 5701636 | tf_op jit(solution)/shard_map/std,dhe->sthe/dot_general | solution.py:67
  163.6 0.6 copy-done.9
  164.3 90.3 %all-reduce.5.cloned.1.call-done = (bf16[4,256,3,384]{3,1,2,0:T(8,128)(2,1)}, bf16[4,128,3,256]{3,1,2,0:T(8,128)(2,1)}) async-done(((bf16[4,256,3,384]{3,1,2,0:T(8,128)(2,1)}, bf16[4,128,3,256]{3,1,2,0:T(8,128)(2,1)}), (bf16[4,256,3,384]{3,1,2,0:T(8,128)(2,1)}, bf16[4,128,3,256]{3,1,2,0:T(8,128)(2,1)})) %all-reduce.5.cloned.1.call-update) | async-done | bytes 3145744 | tf_op jit(solution)/shard_map/psum | solution.py:72
  254.6 1.4 fusion.31
  256.0 1.0 slice.70
  257.1 1.2 slice.71
  258.7 0.9 multiply_reduce_fusion.1
  260.2 0.5 multiply_convert_fusion
  260.6 2.8 fusion
  263.4 5.8 %bitcast_convert_fusion = bf16[4,256,768]{2,1,0:T(8,128)(2,1)} fusion(f32[4,3,256,384]{3,2,1,0:T(8,128)} %get-tuple-element.25, f32[4,384]{1,0:T(4,128)S(1)} %pad_convert_fusion, bf16[4,256,3,128]{3,1,2,0:T(8,128)(2,1)S(1)} %slice.71, bf16[4,128,3,128]{3,1,2,0:T(8,128)(2,1)S(1)} %slice.70, f32[4,256,3]{1,2,0:T(4,128)S(1)} %bitcast.60, ...), kind=kOutput, calls=%fused_computation.5 | convolution fusion | flops 913440768 | bytes 8079360 | tf_op jit(solution)/shard_map/sqhe,hed->sqd/dot_general | solution.py:91
  269.2 32.7 %reduce-scatter.2.cloned.1.call-done = bf16[4,64,768]{2,1,0:T(8,128)(2,1)} async-done(((bf16[4,256,768]{2,1,0:T(8,128)(2,1)}), bf16[4,64,768]{2,1,0:T(8,128)(2,1)}) %reduce-scatter.2.cloned.1.call-update) | async-done | bytes 393232 | tf_op jit(solution)/shard_map/reduce_scatter | solution.py:92
  301.9 1.3 copy.18
  303.2 10.0 %all_to_all.14 = bf16[4,64,768]{2,0,1:T(4,128)(2,1)S(1)} all-to-all(bf16[4,64,768]{2,0,1:T(4,128)(2,1)S(1)} %copy.18), channel_id=1, replica_groups=mesh['batch'=32,'row'=4,'col'=4] {'col'}, dimensions={1} | all-to-all | bytes 786432 | tf_op jit(solution)/shard_map/all_to_all | solution.py:95
  313.2 1.2 copy.26
  314.4 1.5 reshape.111
  316.5 1.4 fusion.46
  318.0 0.9 stack.3
  318.9 15.3 %all-to-all-start.1 = ((f32[32,4,1024]{2,1,0:T(4,128)}), f32[32,4,1024]{2,1,0:T(4,128)S(1)}, u32[]{:S(2)}, u32[]{:S(2)}) async-start(f32[32,4,1024]{2,1,0:T(4,128)} %stack.3), calls=%async_computation.2 | async-start | bytes 1048576 | tf_op jit(solution)/shard_map/all_to_all | solution.py:106
  334.2 1.3 dynamic-slice
  336.4 61.7 %all-reduce.1 = f32[128]{0:T(128)S(1)} all-reduce(f32[128]{0:T(128)S(1)} %dynamic-update-slice), channel_id=1, replica_groups=mesh['batch'=32,'row'=4,'col'=4] {'batch'}, use_global_device_ids=true, to_apply=%add.1 | all-reduce | flops 128 | bytes 1024
  398.2 0.6 gather_fusion.1
  399.0 0.6 gather_fusion
  399.9 0.7 multiply_add_fusion
  (55 shorter events, 2.8 us)
Async XLA Ops:
  6.5 152.0 %copy-start = (bf16[768,3,384]{2,0,1:T(8,128)(2,1)S(1)}, bf16[768,3,384]{2,0,1:T(8,128)(2,1)}, u32[]{:S(2)}) copy-start(bf16[768,3,384]{2,0,1:T(8,128)(2,1)} %param.16) | copy-start | bytes 5308420
  6.5 6.3 %copy-start.1 = (bf16[4,16,3072]{2,1,0:T(8,128)(2,1)S(1)}, bf16[4,16,3072]{2,1,0:T(8,128)(2,1)}, u32[]{:S(2)}) copy-start(bf16[4,16,3072]{2,1,0:T(8,128)(2,1)} %param.13) | copy-start | bytes 1179652
  6.5 73.0 %all-gather.3.cloned.1.call-start = ((), (), s32[]{:S(2)}) async-start(), calls=%async_computation.3 | async-start | bytes 3342336 | tf_op jit(solution)/shard_map/all_gather | solution.py:62
  11.7 146.9 %all-gather.5.cloned.1.call-start = ((), (), s32[]{:S(2)}) async-start(), calls=%async_computation.4 | async-start | bytes 6684672 | tf_op jit(solution)/shard_map/all_gather | solution.py:61
  14.1 240.5 %all-reduce.5.cloned.1.call-start = ((), (), s32[]{:S(2)}) async-start(), calls=%async_computation.6 | async-start | bytes 6291456 | tf_op jit(solution)/shard_map/psum | solution.py:72
  163.5 0.7 copy-start.9
  163.5 0.7 copy-start.5
  163.6 138.4 %reduce-scatter.2.cloned.1.call-start = ((), (), s32[]{:S(2)}) async-start(), calls=%async_computation.5 | async-start | bytes 1966080 | tf_op jit(solution)/shard_map/reduce_scatter | solution.py:92
  254.6 3.7 copy-start.2
  258.7 1.1 copy-start.3
  316.2 20.0 %copy-start.7 = (f32[4]{0:T(128)S(1)}, f32[4]{0:T(128)}, u32[]{:S(2)}) copy-start(f32[4]{0:T(128)} %param.23) | copy-start | bytes 52
  316.2 82.0 %copy-start.8 = (s32[4]{0:T(128)S(1)}, s32[4]{0:T(128)}, u32[]{:S(2)}) copy-start(s32[4]{0:T(128)} %param.22) | copy-start | bytes 52
  316.4 83.4 %copy-start.4 = (f32[4,16,64]{2,1,0:T(8,128)S(1)}, f32[4,16,64]{2,1,0:T(8,128)}, u32[]{:S(2)}) copy-start(f32[4,16,64]{2,1,0:T(8,128)} %param.25) | copy-start | bytes 49156
  316.5 83.4 %copy-start.6 = (f32[4]{0:T(128)S(1)}, f32[4]{0:T(128)}, u32[]{:S(2)}) copy-start(f32[4]{0:T(128)} %param.24) | copy-start | bytes 52
  318.9 80.0 %all-to-all-start.1 = ((f32[32,4,1024]{2,1,0:T(4,128)}), f32[32,4,1024]{2,1,0:T(4,128)S(1)}, u32[]{:S(2)}, u32[]{:S(2)}) async-start(f32[32,4,1024]{2,1,0:T(4,128)} %stack.3), calls=%async_computation.2 | async-start | bytes 1048576 | tf_op jit(solution)/shard_map/all_to_all | solution.py:106
Sparse Core Ops, SparseCore 0:
  11.8 67.7 all-gather.2
  82.6 75.8 all-gather.4
  163.7 90.8 all-reduce.4
  269.3 32.5 reduce-scatter.1
